TPU v7x, 32 devices: a whole 2x2x4 slice. The times are simulated.
32 devices in a mesh: fibre: 2 (over y), chan: 8 (over z, core), tm: 2 (over x).
Axes of the slice: x: 2, y: 2, z: 4, core: 2. Of those that a mesh axis runs over, the one named last changes fastest.
Arguments:
- raw_strain: bfloat16 [2, 2560, 512], P('tm', 'fibre', 'chan'), parts along dimension 1, may hold values from -400 to 400
- fir_taps: bfloat16 [64], replicated, may hold values from -0.75 to 0.75
- live_mask: int32 [2560], P(('fibre', 'chan')), parts along dimension 0, may hold values 0 or 1
Outputs:
- correlations: bfloat16 [2560, 256, 256], P(('fibre', 'chan'), 'tm'), parts along dimension 0
There are 2 independent parts, one for each index of `fibre`. A program takes and returns all parts, laid end to end along the dimension named above; an argument that names none is the same for every part. Nothing has to cross between parts.
All inputs are finite; a program needn't handle non-finite values. No bound on the sum of `live_mask` on one device may be relied on, other than what follows from the above.
Results may differ from a plain program's by a relative error of at most 0.0075.
Values may be sent and summed in bfloat16 or wider, within the bound.
A program may use at most 64 MiB of HBM per device.

v0:
```python
import math

import jax
import jax.numpy as jnp
from jax import lax
from jax.sharding import PartitionSpec as P

OFF = 256
LAG = 128
TAPS = 64
STRIDE = 4
REACH = 2
HIST = 60


def shifted(block, axis, distance):
    devices = range(lax.axis_size(axis))
    route = [(i - distance, i) for i in devices if i - distance in devices]
    return lax.ppermute(block, axis, route)


def decimate(tracts, history, fir_taps):
    window_count, channels, tract_len = tracts.shape
    spans = jnp.concatenate([history, tracts], axis=2)
    total_len = spans.shape[2]
    outputs = tract_len // STRIDE
    grouped = spans.reshape(window_count, channels, total_len // STRIDE, STRIDE)
    reversed_taps = fir_taps[::-1]
    filtered = jnp.zeros((window_count, channels, outputs), jnp.float32)
    for block in range(TAPS // STRIDE):
        filtered = filtered + jnp.einsum(
            "wcns,s->wcn",
            grouped[:, :, block : block + outputs, :],
            reversed_taps[block * STRIDE : (block + 1) * STRIDE],
            preferred_element_type=jnp.float32,
        )
    return filtered.astype(jnp.bfloat16)


def whiten(decimated, live_mask):
    values = decimated.astype(jnp.float32)
    loudness = jnp.sqrt(jnp.mean(values * values, axis=2) + 1e-06)
    alive_flags = live_mask.astype(jnp.float32)
    return (values * (alive_flags[None, :, None] / loudness[:, :, None])).astype(jnp.bfloat16)


def correlate(own_block, extended, lag_start, lag_dev):
    window_count, channels, samples = own_block.shape
    group_size = min(8, channels)
    padded_x = jnp.pad(own_block, ((0, 0), (0, 0), (lag_dev, lag_dev)))
    padded_y = jnp.pad(extended, ((0, 0), (0, 0), (LAG, LAG)))
    span_len = samples + lag_dev
    full_len = samples + 2 * lag_dev
    y_window = lax.dynamic_slice_in_dim(padded_y, lag_start, span_len, 2)
    norm_scale = 1.0 / math.sqrt(samples * window_count)
    partner_rows = group_size + OFF - 1

    def one_group(group_index, result):
        first_chan = group_index * group_size
        chosen = lax.dynamic_slice_in_dim(padded_x, first_chan, group_size, 1)
        repeated = jnp.tile(chosen, (1, 1, lag_dev))
        skewed = repeated[:, :, lag_dev : lag_dev + lag_dev * (full_len - 1)]
        toeplitz = skewed.reshape(window_count, group_size, lag_dev, full_len - 1)[
            :, :, :, :span_len
        ]
        partner = lax.dynamic_slice_in_dim(y_window, first_chan + 1, partner_rows, 1)
        lag_sums = jnp.einsum(
            "wglr,wur->glu", toeplitz, partner, preferred_element_type=jnp.float32
        )
        banded = jnp.stack(
            [lag_sums[member, :, member : member + OFF] for member in range(group_size)], axis=0
        )
        return lax.dynamic_update_slice_in_dim(
            result, (banded * norm_scale).astype(jnp.bfloat16), first_chan, 0
        )

    result = jnp.zeros((channels, lag_dev, OFF), jnp.bfloat16)
    return lax.fori_loop(0, channels // group_size, one_group, result)


def shards(raw_strain, fir_taps, live_mask):
    window_count, channels, tract_len = raw_strain.shape
    turned = lax.all_to_all(raw_strain, "chan", split_axis=1, concat_axis=2, tiled=True)
    no_history = jnp.zeros((window_count, turned.shape[1], HIST), jnp.bfloat16)
    decimated = decimate(turned, no_history, fir_taps)
    whitened_here = whiten(decimated, live_mask)
    whitened = lax.all_gather(whitened_here, "tm", axis=0, tiled=True)
    blocks = [whitened]
    for distance in range(1, REACH + 1):
        blocks.append(shifted(whitened, "chan", -distance))
    extended = jnp.concatenate(blocks, axis=1)
    lag_dev = 2 * LAG // lax.axis_size("tm")
    lag_start = lax.axis_index("tm") * lag_dev
    return correlate(whitened, extended, lag_start, lag_dev)


def solution(mesh):
    placed = (P("tm", "fibre", "chan"), P(), P(("fibre", "chan")))
    return jax.shard_map(
        shards,
        mesh=mesh,
        in_specs=placed,
        out_specs=P(("fibre", "chan"), "tm", None),
        check_vma=False,
    )
```

profile of v0, /device:TPU:1, one launch (start us, length us, event | category | flops | bytes accessed | tf_op | source)
XLA Modules:
  0.0 182.1 jit_solution(3668825591206927714)
XLA Ops:
  1.9 7.5 %reduce.2 = bf16[1280,64]{1,0:T(8,128)(2,1)S(1)} reduce(bf16[1280,1,64]{2,1,0:T(2,128)(2,1)S(1)} %bitcast.201, bf16[]{:T(256)} %broadcast.60), dimensions={1}, to_apply=%bitcast.176.reduce_sub_computation | reduce | bytes 327682
  10.2 6.4 %all-to-all-start = ((bf16[8,2,5120]{2,1,0:T(2,128)(2,1)}), bf16[8,2,5120]{2,1,0:T(2,128)(2,1)S(1)}, u32[]{:S(2)}, u32[]{:S(2)}) async-start(bf16[8,2,5120]{2,1,0:T(2,128)(2,1)} %reshape.165), calls=%async_computation | async-start | bytes 327680 | tf_op jit(solution)/shard_map/all_to_all | solution.py:83
  18.3 4.4 %all-to-all-done = bf16[8,2,5120]{2,1,0:T(2,128)(2,1)S(1)} async-done(((bf16[8,2,5120]{2,1,0:T(2,128)(2,1)}), bf16[8,2,5120]{2,1,0:T(2,128)(2,1)S(1)}, u32[]{:S(2)}, u32[]{:S(2)}) %all-to-all-start) | async-done | bytes 163872 | tf_op jit(solution)/shard_map/all_to_all | solution.py:83
  30.6 3.5 %all-gather = bf16[320,128]{1,0:T(8,128)(2,1)S(1)} all-gather(bf16[160,128]{1,0:T(8,128)(2,1)S(1)} %fusion.29), channel_id=2, replica_groups=mesh['fibre'=2,'chan'=8,'tm'=2] {'tm'}, dimensions={0}, use_global_device_ids=true | all-gather | bytes 122880 | tf_op jit(solution)/shard_map/all_gather | solution.py:87
  35.4 4.4 %collective-permute-start = (bf16[2,160,128]{2,1,0:T(8,128)(2,1)S(1)}, bf16[2,160,128]{2,1,0:T(8,128)(2,1)S(1)}, u32[]{:S(2)}, u32[]{:S(2)}) collective-permute-start(bf16[2,160,128]{2,1,0:T(8,128)(2,1)S(1)} %bitcast.206), channel_id=1, source_target_pairs={{2,0},{4,2},{6,4},{8,6},{10,8},{12,10},{14,12},{3,1},{5,3},{7,5},{... | collective-permute-start | bytes 245768 | tf_op jit(solution)/shard_map/ppermute | solution.py:19
  39.8 4.1 %collective-permute-done = bf16[2,160,128]{2,1,0:T(8,128)(2,1)S(1)} collective-permute-done((bf16[2,160,128]{2,1,0:T(8,128)(2,1)S(1)}, bf16[2,160,128]{2,1,0:T(8,128)(2,1)S(1)}, u32[]{:S(2)}, u32[]{:S(2)}) %collective-permute-start) | collective-permute-done | bytes 81952 | tf_op jit(solution)/shard_map/ppermute | solution.py:19
  45.1 5.4 %broadcast_in_dim.2.clone = bf16[160,128,256]{2,1,0:T(8,128)(2,1)} broadcast(bf16[]{:T(256)} %constant.76.clone.1), dimensions={} | broadcast | bytes 10485762 | tf_op jit(solution)/shard_map/broadcast_in_dim | solution.py:77
  50.5 131.6 %while.15 = (s32[]{:T(128)}, bf16[160,128,256]{2,1,0:T(8,128)(2,1)}, bf16[2,160,384]{2,1,0:T(8,128)(2,1)S(1)}, bf16[2,480,256]{2,1,0:T(8,128)(2,1)}, s32[]{:T(12...) while((s32[]{:T(128)}, bf16[160,128,256]{2,1,0:T(8,128)(2,1)}, bf16[2,160,384]{2,1,0:T(8,128)(2,1)S(1)}, ...), condition=%wide.region_2.3_spmd, body=%wide.region_1.2_spmd.sunk | while | flops 276299776 | bytes 16048325 | solution.py:78
  50.8 3.5 %reshape.168 = bf16[2,8,128,383]{3,2,1,0:T(8,128)(2,1)S(1)} reshape(bf16[2,8,49024]{2,1,0:T(8,128)(2,1)S(1)} %slice.395) | data formatting | bytes 3137536 | tf_op jit(solution)/shard_map/while/body/eval_jaxpr/reshape | solution.py:63
  57.4 3.5 %reshape.168 = bf16[2,8,128,383]{3,2,1,0:T(8,128)(2,1)S(1)} reshape(bf16[2,8,49024]{2,1,0:T(8,128)(2,1)S(1)} %slice.395) | data formatting | bytes 3137536 | tf_op jit(solution)/shard_map/while/body/eval_jaxpr/reshape | solution.py:63
  64.0 3.5 %reshape.168 = bf16[2,8,128,383]{3,2,1,0:T(8,128)(2,1)S(1)} reshape(bf16[2,8,49024]{2,1,0:T(8,128)(2,1)S(1)} %slice.395) | data formatting | bytes 3137536 | tf_op jit(solution)/shard_map/while/body/eval_jaxpr/reshape | solution.py:63
  70.5 3.5 %reshape.168 = bf16[2,8,128,383]{3,2,1,0:T(8,128)(2,1)S(1)} reshape(bf16[2,8,49024]{2,1,0:T(8,128)(2,1)S(1)} %slice.395) | data formatting | bytes 3137536 | tf_op jit(solution)/shard_map/while/body/eval_jaxpr/reshape | solution.py:63
  77.1 3.5 %reshape.168 = bf16[2,8,128,383]{3,2,1,0:T(8,128)(2,1)S(1)} reshape(bf16[2,8,49024]{2,1,0:T(8,128)(2,1)S(1)} %slice.395) | data formatting | bytes 3137536 | tf_op jit(solution)/shard_map/while/body/eval_jaxpr/reshape | solution.py:63
  80.7 1.5 convolution_bitcast_fusion.2
  83.7 3.5 %reshape.168 = bf16[2,8,128,383]{3,2,1,0:T(8,128)(2,1)S(1)} reshape(bf16[2,8,49024]{2,1,0:T(8,128)(2,1)S(1)} %slice.395) | data formatting | bytes 3137536 | tf_op jit(solution)/shard_map/while/body/eval_jaxpr/reshape | solution.py:63
  90.3 3.5 %reshape.168 = bf16[2,8,128,383]{3,2,1,0:T(8,128)(2,1)S(1)} reshape(bf16[2,8,49024]{2,1,0:T(8,128)(2,1)S(1)} %slice.395) | data formatting | bytes 3137536 | tf_op jit(solution)/shard_map/while/body/eval_jaxpr/reshape | solution.py:63
  96.9 3.5 %reshape.168 = bf16[2,8,128,383]{3,2,1,0:T(8,128)(2,1)S(1)} reshape(bf16[2,8,49024]{2,1,0:T(8,128)(2,1)S(1)} %slice.395) | data formatting | bytes 3137536 | tf_op jit(solution)/shard_map/while/body/eval_jaxpr/reshape | solution.py:63
  100.4 1.5 convolution_bitcast_fusion.2
  103.4 3.5 %reshape.168 = bf16[2,8,128,383]{3,2,1,0:T(8,128)(2,1)S(1)} reshape(bf16[2,8,49024]{2,1,0:T(8,128)(2,1)S(1)} %slice.395) | data formatting | bytes 3137536 | tf_op jit(solution)/shard_map/while/body/eval_jaxpr/reshape | solution.py:63
  110.0 3.5 %reshape.168 = bf16[2,8,128,383]{3,2,1,0:T(8,128)(2,1)S(1)} reshape(bf16[2,8,49024]{2,1,0:T(8,128)(2,1)S(1)} %slice.395) | data formatting | bytes 3137536 | tf_op jit(solution)/shard_map/while/body/eval_jaxpr/reshape | solution.py:63
  116.6 3.5 %reshape.168 = bf16[2,8,128,383]{3,2,1,0:T(8,128)(2,1)S(1)} reshape(bf16[2,8,49024]{2,1,0:T(8,128)(2,1)S(1)} %slice.395) | data formatting | bytes 3137536 | tf_op jit(solution)/shard_map/while/body/eval_jaxpr/reshape | solution.py:63
  123.2 3.5 %reshape.168 = bf16[2,8,128,383]{3,2,1,0:T(8,128)(2,1)S(1)} reshape(bf16[2,8,49024]{2,1,0:T(8,128)(2,1)S(1)} %slice.395) | data formatting | bytes 3137536 | tf_op jit(solution)/shard_map/while/body/eval_jaxpr/reshape | solution.py:63
  129.8 3.5 %reshape.168 = bf16[2,8,128,383]{3,2,1,0:T(8,128)(2,1)S(1)} reshape(bf16[2,8,49024]{2,1,0:T(8,128)(2,1)S(1)} %slice.395) | data formatting | bytes 3137536 | tf_op jit(solution)/shard_map/while/body/eval_jaxpr/reshape | solution.py:63
  133.3 1.5 convolution_bitcast_fusion.2
  136.3 3.5 %reshape.168 = bf16[2,8,128,383]{3,2,1,0:T(8,128)(2,1)S(1)} reshape(bf16[2,8,49024]{2,1,0:T(8,128)(2,1)S(1)} %slice.395) | data formatting | bytes 3137536 | tf_op jit(solution)/shard_map/while/body/eval_jaxpr/reshape | solution.py:63
  142.9 3.5 %reshape.168 = bf16[2,8,128,383]{3,2,1,0:T(8,128)(2,1)S(1)} reshape(bf16[2,8,49024]{2,1,0:T(8,128)(2,1)S(1)} %slice.395) | data formatting | bytes 3137536 | tf_op jit(solution)/shard_map/while/body/eval_jaxpr/reshape | solution.py:63
  149.5 3.5 %reshape.168 = bf16[2,8,128,383]{3,2,1,0:T(8,128)(2,1)S(1)} reshape(bf16[2,8,49024]{2,1,0:T(8,128)(2,1)S(1)} %slice.395) | data formatting | bytes 3137536 | tf_op jit(solution)/shard_map/while/body/eval_jaxpr/reshape | solution.py:63
  153.0 1.5 convolution_bitcast_fusion.2
  156.1 3.5 %reshape.168 = bf16[2,8,128,383]{3,2,1,0:T(8,128)(2,1)S(1)} reshape(bf16[2,8,49024]{2,1,0:T(8,128)(2,1)S(1)} %slice.395) | data formatting | bytes 3137536 | tf_op jit(solution)/shard_map/while/body/eval_jaxpr/reshape | solution.py:63
  162.7 3.5 %reshape.168 = bf16[2,8,128,383]{3,2,1,0:T(8,128)(2,1)S(1)} reshape(bf16[2,8,49024]{2,1,0:T(8,128)(2,1)S(1)} %slice.395) | data formatting | bytes 3137536 | tf_op jit(solution)/shard_map/while/body/eval_jaxpr/reshape | solution.py:63
  169.2 3.5 %reshape.168 = bf16[2,8,128,383]{3,2,1,0:T(8,128)(2,1)S(1)} reshape(bf16[2,8,49024]{2,1,0:T(8,128)(2,1)S(1)} %slice.395) | data formatting | bytes 3137536 | tf_op jit(solution)/shard_map/while/body/eval_jaxpr/reshape | solution.py:63
  175.8 3.5 %reshape.168 = bf16[2,8,128,383]{3,2,1,0:T(8,128)(2,1)S(1)} reshape(bf16[2,8,49024]{2,1,0:T(8,128)(2,1)S(1)} %slice.395) | data formatting | bytes 3137536 | tf_op jit(solution)/shard_map/while/body/eval_jaxpr/reshape | solution.py:63
  (365 shorter events, 67.6 us)
Async XLA Ops:
  0.0 16.6 %copy-start = (bf16[64]{0:T(256)(128)(2,1)S(1)}, bf16[64]{0:T(256)(128)(2,1)}, u32[]{:S(2)}) copy-start(bf16[64]{0:T(256)(128)(2,1)} %param.6) | copy-start | bytes 388
  10.2 12.4 %all-to-all-start = ((bf16[8,2,5120]{2,1,0:T(2,128)(2,1)}), bf16[8,2,5120]{2,1,0:T(2,128)(2,1)S(1)}, u32[]{:S(2)}, u32[]{:S(2)}) async-start(bf16[8,2,5120]{2,1,0:T(2,128)(2,1)} %reshape.165), calls=%async_computation | async-start | bytes 327680 | tf_op jit(solution)/shard_map/all_to_all | solution.py:83
  29.4 1.1 copy-start.1
  34.1 5.7 %collective-permute-start.1 = (bf16[2,160,128]{2,1,0:T(8,128)(2,1)S(1)}, bf16[2,160,128]{2,1,0:T(8,128)(2,1)S(1)}, u32[]{:S(2)}, u32[]{:S(2)}) collective-permute-start(bf16[2,160,128]{2,1,0:T(8,128)(2,1)S(1)} %bitcast.205), channel_id=1, source_target_pairs={{4,0},{6,2},{8,4},{10,6},{12,8},{14,10},{5,1},{7,3},{9,5},{11,7},{... | collective-permute-start | bytes 245768 | tf_op jit(solution)/shard_map/ppermute | solution.py:19
  35.4 8.6 %collective-permute-start = (bf16[2,160,128]{2,1,0:T(8,128)(2,1)S(1)}, bf16[2,160,128]{2,1,0:T(8,128)(2,1)S(1)}, u32[]{:S(2)}, u32[]{:S(2)}) collective-permute-start(bf16[2,160,128]{2,1,0:T(8,128)(2,1)S(1)} %bitcast.206), channel_id=1, source_target_pairs={{2,0},{4,2},{6,4},{8,6},{10,8},{12,10},{14,12},{3,1},{5,3},{7,5},{... | collective-permute-start | bytes 245768 | tf_op jit(solution)/shard_map/ppermute | solution.py:19
where the time goes:
time: 183 us; the launch traced here: 182 us
  local copies, waits for them, and re-layouts  111 us (61%)
  matrix products  33.6 us (18%)
  starting transfers between devices  12 us (7%)
  other arithmetic  10.7 us (6%)
  waiting for transfers between devices  8.51 us (5%)
  blocking collectives  3.52 us (2%)
  loops' own time  2.11 us (1%)
    reshape x20, local copies, waits for them, and re-layouts, one_group(): skewed.reshape(window_count, group_size, lag_dev, full_len - 1)  70.8 us
    dot_general x20, matrix products, one_group(): jnp.einsum('wglr,wur->glu', toeplitz, partner, preferred_element_type=jnp...  29 us
    dynamic_update_slice x40, local copies, waits for them, and re-layouts, one_group(): lax.dynamic_update_slice_in_dim(result, (banded * norm_scale).astype(jnp....  20.9 us
    unnamed x1, other arithmetic  7.45 us
    all_to_all x1, starting transfers between devices, shards(): lax.all_to_all(raw_strain, 'chan', split_axis=1, concat_axis=2, tiled=True)  6.37 us
    ppermute x2, starting transfers between devices, shifted(): return lax.ppermute(block, axis, route)  5.67 us
    broadcast_in_dim x1, local copies, waits for them, and re-layouts, correlate(): result = jnp.zeros((channels, lag_dev, OFF), jnp.bfloat16)  5.4 us
    dot_general x16, matrix products, decimate(): jnp.einsum('wcns,s->wcn', grouped[:, :, block:block + outputs, :], revers...  4.57 us
  transfers between devices with their start and end apart: 3, of which 2 were waited for; matrix products, arithmetic and copies ran while one was open for 1% of the time, Pallas kernels for 0%

commit v1 on v0

v1 whole, which is shorter than its diff:
```python
import functools
import math

import jax
import jax.numpy as jnp
from jax import lax
from jax.experimental import pallas as pl
from jax.experimental.pallas import tpu as pltpu
from jax.sharding import PartitionSpec as P

OFF = 256
LAG = 128
TAPS = 64
STRIDE = 4
HIST = 60
LANES = 128
SUB = 16
MESH = pl.DeviceIdType.MESH


def tap_block(taps_row, member, members, tract_len, rows):
    width = members * tract_len
    tap = lax.broadcasted_iota(jnp.int32, (TAPS, width), 0)
    lane = lax.broadcasted_iota(jnp.int32, (TAPS, width), 1)
    flip = jnp.where(tap + lane == TAPS - 1, 1.0, 0.0).astype(jnp.bfloat16)
    reversed_row = jnp.dot(
        jnp.broadcast_to(taps_row, (8, TAPS)), flip, preferred_element_type=jnp.float32
    )[0:1]
    start = (member * tract_len - HIST) % width
    rolled = pltpu.roll(
        jnp.broadcast_to(reversed_row, (rows, width)), start, 1, stride=STRIDE, stride_axis=0
    )
    row = lax.broadcasted_iota(jnp.int32, (rows, width), 0)
    local = lax.broadcasted_iota(jnp.int32, (rows, width), 1) - member * tract_len
    index = STRIDE * row + STRIDE - 1 - local
    keep = (local >= 0) & (local < tract_len) & (index >= 0) & (index < TAPS)
    return jnp.where(keep, rolled, 0.0).astype(jnp.bfloat16)


def prepare_kernel(
    n_chan,
    n_tm,
    members,
    raw_ref,
    taps_ref,
    mask_ref,
    out_ref,
    packed,
    received,
    fir,
    white,
    extended,
    send_a,
    recv_a,
    send_b,
    recv_b,
):
    me = lax.axis_index("chan")
    my_tm = lax.axis_index("tm")
    tract_len = raw_ref.shape[2]
    channels, samples = white.shape
    part = channels // members
    width = members * tract_len
    outputs = tract_len // STRIDE
    reach = -(-OFF // channels)

    barrier = pltpu.get_barrier_semaphore()
    for step in range(n_chan):
        for turn in range(n_tm):
            if step or turn:
                pl.semaphore_signal(
                    barrier,
                    inc=1,
                    device_id={
                        "chan": lax.rem(me + step, n_chan),
                        "tm": lax.rem(my_tm + turn, n_tm),
                    },
                    device_id_type=MESH,
                )
    for block in range(n_chan):
        pieces = [
            raw_ref[0, block * channels + m * part : block * channels + (m + 1) * part, :]
            for m in range(members)
        ]
        packed[block] = jnp.concatenate(pieces, axis=1)
    pl.semaphore_wait(barrier, n_chan * n_tm - 1)

    spread = []
    for step in range(1, n_chan):
        copy = pltpu.make_async_remote_copy(
            src_ref=packed.at[lax.rem(me + step, n_chan)],
            dst_ref=received.at[me],
            send_sem=send_a.at[step],
            recv_sem=recv_a.at[step],
            device_id={"chan": lax.rem(me + step, n_chan)},
            device_id_type=MESH,
        )
        copy.start()
        spread.append(copy)
    received[me] = packed[me]

    fir[...] = jnp.zeros_like(fir)
    taps_row = taps_ref[...]
    rows = 2 * outputs
    for m in range(members):
        block = tap_block(taps_row, m, members, tract_len, rows)
        for source in range(n_chan):
            first = m * samples + source * outputs
            count = min(rows, samples - source * outputs)
            fir[first : first + count, source * width : (source + 1) * width] = block[:count]
    alive = mask_ref[...].astype(jnp.float32)
    diagonal = lax.broadcasted_iota(jnp.int32, (channels, channels), 0) == lax.broadcasted_iota(
        jnp.int32, (channels, channels), 1
    )
    alive_column = jnp.sum(
        jnp.where(diagonal, jnp.broadcast_to(alive, (channels, channels)), 0.0),
        axis=1,
        keepdims=True,
    )
    for k in range(1, reach + 1):
        count = min(channels, OFF - (k - 1) * channels)

        @pl.when(me + k >= n_chan)
        def _():
            extended[k * channels : k * channels + count, :] = jnp.zeros(
                (count, extended.shape[1]), extended.dtype
            )

    for copy in spread:
        copy.wait_recv()
    tracts = jnp.concatenate([received[d] for d in range(n_chan)], axis=1)
    filtered = lax.dot_general(
        tracts, fir[...], (((1,), (1,)), ((), ())), preferred_element_type=jnp.float32
    )
    for m in range(members):
        decimated = filtered[:, m * samples : (m + 1) * samples]
        decimated = decimated.astype(jnp.bfloat16).astype(jnp.float32)
        loudness = jnp.sqrt(jnp.mean(decimated * decimated, axis=1, keepdims=True) + 1e-06)
        gain = alive_column[m * part : (m + 1) * part] / loudness
        white[m * part : (m + 1) * part, :] = (decimated * gain).astype(jnp.bfloat16)

    def share(k, turn):
        count = channels if k == 0 else min(channels, OFF - (k - 1) * channels)
        window = pl.multiple_of(my_tm * samples, LANES)
        return pltpu.make_async_remote_copy(
            src_ref=white.at[pl.ds(0, count), :],
            dst_ref=extended.at[pl.ds(k * channels, count), pl.ds(window, samples)],
            send_sem=send_b.at[k, turn],
            recv_sem=recv_b.at[k, turn],
            device_id={"chan": me - k, "tm": lax.rem(my_tm + turn, n_tm)},
            device_id_type=MESH,
        )

    pairs = [(k, t) for k in range(reach, -1, -1) for t in range(n_tm - 1, -1, -1) if k or t]
    for k, turn in pairs:

        @pl.when(me >= k)
        def _():
            share(k, turn).start()

    own = pl.multiple_of(my_tm * samples, LANES)
    extended[0:channels, pl.ds(own, samples)] = white[...]
    for copy in spread:
        copy.wait_send()
    for k, turn in pairs:

        @pl.when(me + k < n_chan)
        def _():
            share(k, turn).wait_recv()

        @pl.when(me >= k)
        def _():
            share(k, turn).wait_send()

    out_ref[...] = extended[...]


def prepare(raw_strain, fir_taps, live_mask, n_chan, n_tm):
    _, all_channels, tract_len = raw_strain.shape
    channels = all_channels // n_chan
    samples = tract_len * n_chan // STRIDE
    members = max(1, LANES // tract_len)
    part = channels // members
    width = members * tract_len
    reach = -(-OFF // channels)
    vmem = pl.BlockSpec(memory_space=pltpu.VMEM)
    return pl.pallas_call(
        functools.partial(prepare_kernel, n_chan, n_tm, members),
        out_shape=jax.ShapeDtypeStruct((channels + OFF, n_tm * samples), jnp.bfloat16),
        in_specs=[vmem, vmem, vmem],
        out_specs=vmem,
        scratch_shapes=[
            pltpu.VMEM((n_chan, part, width), jnp.bfloat16),
            pltpu.VMEM((n_chan, part, width), jnp.bfloat16),
            pltpu.VMEM((members * samples, n_chan * width), jnp.bfloat16),
            pltpu.VMEM((channels, samples), jnp.bfloat16),
            pltpu.VMEM((channels + OFF, n_tm * samples), jnp.bfloat16),
            pltpu.SemaphoreType.DMA((n_chan,)),
            pltpu.SemaphoreType.DMA((n_chan,)),
            pltpu.SemaphoreType.DMA((reach + 1, n_tm)),
            pltpu.SemaphoreType.DMA((reach + 1, n_tm)),
        ],
        compiler_params=pltpu.CompilerParams(collective_id=0, has_side_effects=True),
        name="prepare",
    )(raw_strain, fir_taps.reshape(1, TAPS), live_mask.reshape(1, channels))


def correlate_kernel(windows, samples, lag_dev, ext_ref, out_ref, wide, shifted):
    phase = pl.program_id(0)
    groups = out_ref.shape[0]
    rows = ext_ref.shape[0]
    first_lag = lax.axis_index("tm") * lag_dev - LAG
    norm_scale = 1.0 / math.sqrt(samples * windows)

    @pl.when(phase == 0)
    def _():
        wide[0:rows, :] = ext_ref[...].astype(jnp.float32)
        wide[rows : rows + 8, :] = jnp.zeros((8, wide.shape[1]), jnp.float32)

    chosen = [wide[g * SUB : g * SUB + 1, :] for g in range(groups)]
    moved = wide[1 : rows + 1, :]
    shifted[...] = moved[: shifted.shape[0]].astype(jnp.bfloat16)
    wide[0:rows, :] = moved
    lag = first_lag + lax.broadcasted_iota(jnp.int32, (lag_dev, samples), 0)
    at = lax.broadcasted_iota(jnp.int32, (lag_dev, samples), 1) - lag
    keep = (at >= 0) & (at < samples)
    if lag_dev % samples == 0 and LAG % samples == 0:
        turn = None
    else:
        turn = lax.rem(first_lag + samples * (-(-LAG // samples)), samples)
    for g in range(groups):
        row = chosen[g]
        parts = []
        for w in range(windows):
            trace = row[:, w * samples : (w + 1) * samples]
            if turn is not None:
                trace = pltpu.roll(jnp.broadcast_to(trace, (8, samples)), turn, 1)[0:1]
            trace = jnp.broadcast_to(trace, (lag_dev, samples))
            rolled = pltpu.roll(trace, 0, 1, stride=1, stride_axis=0)
            parts.append(jnp.where(keep, rolled, 0.0).astype(jnp.bfloat16))
        toeplitz = jnp.concatenate(parts, axis=1)
        sums = lax.dot_general(
            toeplitz,
            shifted[g * SUB : g * SUB + OFF, :],
            (((1,), (1,)), ((), ())),
            preferred_element_type=jnp.float32,
        )
        out_ref[g, 0] = (sums * norm_scale).astype(jnp.bfloat16)


def correlate(extended, channels, windows, lag_dev):
    depth = extended.shape[1]
    samples = depth // windows
    groups = channels // SUB
    out = pl.pallas_call(
        functools.partial(correlate_kernel, windows, samples, lag_dev),
        out_shape=jax.ShapeDtypeStruct((groups, SUB, lag_dev, OFF), jnp.bfloat16),
        grid=(SUB,),
        in_specs=[pl.BlockSpec(extended.shape, lambda r: (0, 0))],
        out_specs=pl.BlockSpec((groups, 1, lag_dev, OFF), lambda r: (0, r, 0, 0)),
        scratch_shapes=[
            pltpu.VMEM((extended.shape[0] + 8, depth), jnp.float32),
            pltpu.VMEM(((groups - 1) * SUB + OFF, depth), jnp.bfloat16),
        ],
        name="correlate",
    )(extended)
    return out.reshape(channels, lag_dev, OFF)


def shards(raw_strain, fir_taps, live_mask):
    n_chan = lax.axis_size("chan")
    n_tm = lax.axis_size("tm")
    extended = prepare(raw_strain, fir_taps, live_mask, n_chan, n_tm)
    return correlate(extended, live_mask.shape[0], n_tm, 2 * LAG // n_tm)


def solution(mesh):
    placed = (P("tm", "fibre", "chan"), P(), P(("fibre", "chan")))
    return jax.shard_map(
        shards,
        mesh=mesh,
        in_specs=placed,
        out_specs=P(("fibre", "chan"), "tm", None),
        check_vma=False,
    )
```

time: 183 us -> 30.7 us (0.17)
  local copies, waits for them, and re-layouts: 111 us -> 1.81 us
  matrix products: 33.6 us -> 0 us
  Pallas kernels: 0 us -> 28.7 us
  starting transfers between devices: 12 us -> 0 us
  other arithmetic: 10.7 us -> 0 us
  waiting for transfers between devices: 8.51 us -> 0 us
  blocking collectives: 3.52 us -> 0 us
  loops' own time: 2.11 us -> 0 us
    reshape x21 -> x0, local copies, waits for them, and re-layouts: 70.9 us -> none  [the longest x20 70.8 us: one_group(): skewed.reshape(window_count, group_size, lag_dev, full_len - 1)]
    dot_general x36 -> x0, matrix products: 33.6 us -> none  [the longest x20 29 us: one_group(): jnp.einsum('wglr,wur->glu', toeplitz, partner, preferred_element_type=jnp...]
    pallas_call x0 -> x2, Pallas kernels: none -> 28.7 us  [the longest x1 15.9 us: prepare(): pl.pallas_call(functools.partial(prepare_kernel, n_chan, n_tm, members),...]
    dynamic_update_slice x40 -> x0, local copies, waits for them, and re-layouts: 20.9 us -> none  [one_group(): lax.dynamic_update_slice_in_dim(result, (banded * norm_scale).astype(jnp....]
    unnamed x1 -> x0, other arithmetic: 7.45 us -> none
    all_to_all x1 -> x0, starting transfers between devices: 6.37 us -> none  [shards(): lax.all_to_all(raw_strain, 'chan', split_axis=1, concat_axis=2, tiled=True)]
    ppermute x2 -> x0, starting transfers between devices: 5.67 us -> none  [shifted(): return lax.ppermute(block, axis, route)]
    broadcast_in_dim x1 -> x0, local copies, waits for them, and re-layouts: 5.4 us -> none  [correlate(): result = jnp.zeros((channels, lag_dev, OFF), jnp.bfloat16)]
  transfers between devices with their start and end apart: 3 -> 0, of which waited for: 2 -> 0; matrix products, arithmetic and copies ran while one was open for 1% -> 0% of each run, Pallas kernels for 0% -> 0%
where the time goes in v1:
time: 30.7 us; the launch traced here: 30.5 us
  Pallas kernels  28.7 us (93%)
  local copies, waits for them, and re-layouts  1.81 us (6%)
    pallas_call x1, Pallas kernels, prepare(): pl.pallas_call(functools.partial(prepare_kernel, n_chan, n_tm, members),...  15.9 us
    pallas_call x1, Pallas kernels, correlate(): pl.pallas_call(functools.partial(correlate_kernel, windows, samples, lag_...  12.8 us
    unnamed x1, local copies, waits for them, and re-layouts  1.81 us

profile of v1, /device:TPU:1, one launch (start us, length us, event | category | flops | bytes accessed | tf_op | source)
XLA Modules:
  0.0 30.5 jit_solution(10488946476366142175)
XLA Ops:
  0.0 1.8 %copy.4.raw_ref = bf16[1,1280,64]{2,1,0:T(8,128)(2,1)} copy(bf16[1,1280,64]{1,2,0:T(8,128)(2,1)} %param.3) | data formatting | bytes 327680 | tf_op args[0]
  1.8 15.9 %prepare.1.ext_ref = bf16[416,256]{1,0:T(8,128)(2,1)} custom-call(bf16[1,1280,64]{2,1,0:T(8,128)(2,1)} %copy.4.raw_ref, bf16[1,64]{1,0:T(2,128)(2,1)} %bitcast.4, s32[1,160]{1,0:T(1,128)} %bitcast.3), custom_call_target="tpu_custom_call" | custom-call | tf_op jit(solution)/shard_map/prepare/pallas_call | solution.py:187
  17.7 12.8 %correlate.1 = bf16[10,16,128,256]{3,2,1,0:T(8,128)(2,1)} custom-call(bf16[416,256]{1,0:T(8,128)(2,1)} %prepare.1.ext_ref), custom_call_target="tpu_custom_call" | custom-call | tf_op jit(solution)/shard_map/correlate/pallas_call | solution.py:255

commit v2 on v1

--- a/solution.py
+++ b/solution.py
@@ -57,7 +57,7 @@
 ):
     me = lax.axis_index("chan")
     my_tm = lax.axis_index("tm")
-    tract_len = raw_ref.shape[2]
+    tract_len = raw_ref.shape[1]
     channels, samples = white.shape
     part = channels // members
     width = members * tract_len
@@ -77,11 +77,10 @@
                     },
                     device_id_type=MESH,
                 )
+    turned = raw_ref[0].astype(jnp.float32).T.astype(jnp.bfloat16)
     for block in range(n_chan):
-        pieces = [
-            raw_ref[0, block * channels + m * part : block * channels + (m + 1) * part, :]
-            for m in range(members)
-        ]
+        first = block * channels
+        pieces = [turned[first + m * part : first + (m + 1) * part] for m in range(members)]
         packed[block] = jnp.concatenate(pieces, axis=1)
     pl.semaphore_wait(barrier, n_chan * n_tm - 1)
 
@@ -202,69 +201,74 @@
         ],
         compiler_params=pltpu.CompilerParams(collective_id=0, has_side_effects=True),
         name="prepare",
-    )(raw_strain, fir_taps.reshape(1, TAPS), live_mask.reshape(1, channels))
-
-
-def correlate_kernel(windows, samples, lag_dev, ext_ref, out_ref, wide, shifted):
-    phase = pl.program_id(0)
-    groups = out_ref.shape[0]
-    rows = ext_ref.shape[0]
+    )(raw_strain.transpose(0, 2, 1), fir_taps.reshape(1, TAPS), live_mask.reshape(1, channels))
+
+
+def correlate_kernel(windows, samples, lag_dev, ext_ref, out_ref, wide):
+    group = pl.program_id(0)
     first_lag = lax.axis_index("tm") * lag_dev - LAG
     norm_scale = 1.0 / math.sqrt(samples * windows)
-
-    @pl.when(phase == 0)
+    rows = ext_ref.shape[0]
+
+    @pl.when(group == 0)
     def _():
-        wide[0:rows, :] = ext_ref[...].astype(jnp.float32)
-        wide[rows : rows + 8, :] = jnp.zeros((8, wide.shape[1]), jnp.float32)
-
-    chosen = [wide[g * SUB : g * SUB + 1, :] for g in range(groups)]
-    moved = wide[1 : rows + 1, :]
-    shifted[...] = moved[: shifted.shape[0]].astype(jnp.bfloat16)
-    wide[0:rows, :] = moved
+        wide[0:rows, :] = ext_ref[...]
+        wide[rows:, :] = jnp.zeros((wide.shape[0] - rows, wide.shape[1]), wide.dtype)
+
+    base = pl.multiple_of(group * SUB, SUB)
+    own = wide[pl.ds(base, SUB), :].astype(jnp.float32)
+    partners = wide[pl.ds(base, OFF), :]
+    beyond = wide[pl.ds(pl.multiple_of(base + OFF, SUB), LANES), :]
     lag = first_lag + lax.broadcasted_iota(jnp.int32, (lag_dev, samples), 0)
     at = lax.broadcasted_iota(jnp.int32, (lag_dev, samples), 1) - lag
     keep = (at >= 0) & (at < samples)
+    lane = lax.broadcasted_iota(jnp.int32, (lag_dev, LANES), 1)
     if lag_dev % samples == 0 and LAG % samples == 0:
         turn = None
     else:
         turn = lax.rem(first_lag + samples * (-(-LAG // samples)), samples)
-    for g in range(groups):
-        row = chosen[g]
+    blocks = []
+    for r in range(SUB):
         parts = []
         for w in range(windows):
-            trace = row[:, w * samples : (w + 1) * samples]
+            trace = own[r : r + 1, w * samples : (w + 1) * samples]
             if turn is not None:
                 trace = pltpu.roll(jnp.broadcast_to(trace, (8, samples)), turn, 1)[0:1]
             trace = jnp.broadcast_to(trace, (lag_dev, samples))
             rolled = pltpu.roll(trace, 0, 1, stride=1, stride_axis=0)
             parts.append(jnp.where(keep, rolled, 0.0).astype(jnp.bfloat16))
-        toeplitz = jnp.concatenate(parts, axis=1)
-        sums = lax.dot_general(
-            toeplitz,
-            shifted[g * SUB : g * SUB + OFF, :],
-            (((1,), (1,)), ((), ())),
-            preferred_element_type=jnp.float32,
-        )
-        out_ref[g, 0] = (sums * norm_scale).astype(jnp.bfloat16)
+        blocks.append(jnp.concatenate(parts, axis=1))
+    toeplitz = jnp.concatenate(blocks, axis=0)
+    contract = (((1,), (1,)), ((), ()))
+    near = lax.dot_general(toeplitz, partners, contract, preferred_element_type=jnp.float32)
+    far = lax.dot_general(toeplitz, beyond, contract, preferred_element_type=jnp.float32)
+    for r in range(SUB):
+        first = r * lag_dev
+        skip = r + 1
+        columns = [
+            near[first : first + lag_dev, k * LANES : (k + 1) * LANES] for k in range(OFF // LANES)
+        ]
+        columns[0] = jnp.where(lane < skip, far[first : first + lag_dev], columns[0])
+        columns = [(c * norm_scale).astype(jnp.bfloat16).astype(jnp.float32) for c in columns]
+        turned = [pltpu.roll(column, LANES - skip, 1) for column in columns]
+        for k in range(len(columns)):
+            following = turned[(k + 1) % len(columns)]
+            value = jnp.where(lane < LANES - skip, turned[k], following)
+            out_ref[r, :, k * LANES : (k + 1) * LANES] = value.astype(jnp.bfloat16)
 
 
 def correlate(extended, channels, windows, lag_dev):
     depth = extended.shape[1]
     samples = depth // windows
-    groups = channels // SUB
-    out = pl.pallas_call(
+    return pl.pallas_call(
         functools.partial(correlate_kernel, windows, samples, lag_dev),
-        out_shape=jax.ShapeDtypeStruct((groups, SUB, lag_dev, OFF), jnp.bfloat16),
-        grid=(SUB,),
-        in_specs=[pl.BlockSpec(extended.shape, lambda r: (0, 0))],
-        out_specs=pl.BlockSpec((groups, 1, lag_dev, OFF), lambda r: (0, r, 0, 0)),
-        scratch_shapes=[
-            pltpu.VMEM((extended.shape[0] + 8, depth), jnp.float32),
-            pltpu.VMEM(((groups - 1) * SUB + OFF, depth), jnp.bfloat16),
-        ],
+        out_shape=jax.ShapeDtypeStruct((channels, lag_dev, OFF), jnp.bfloat16),
+        grid=(channels // SUB,),
+        in_specs=[pl.BlockSpec(extended.shape, lambda g: (0, 0))],
+        out_specs=pl.BlockSpec((SUB, lag_dev, OFF), lambda g: (g, 0, 0)),
+        scratch_shapes=[pltpu.VMEM((channels - SUB + OFF + LANES, depth), jnp.bfloat16)],
         name="correlate",
     )(extended)
-    return out.reshape(channels, lag_dev, OFF)
 
 
 def shards(raw_strain, fir_taps, live_mask):

time: 30.7 us -> 26.9 us (0.88)
  Pallas kernels: 28.7 us -> 26.8 us
  local copies, waits for them, and re-layouts: 1.81 us -> 0 us
    pallas_call x1, Pallas kernels: 12.8 us -> 10.9 us  [correlate(): pl.pallas_call(functools.partial(correlate_kernel, windows, samples, lag_...]
    unnamed x1 -> x0, local copies, waits for them, and re-layouts: 1.81 us -> none
where the time goes in v2:
time: 26.9 us; the launch traced here: 26.8 us
  Pallas kernels  26.8 us (100%)
    pallas_call x1, Pallas kernels, prepare(): pl.pallas_call(functools.partial(prepare_kernel, n_chan, n_tm, members),...  15.8 us
    pallas_call x1, Pallas kernels, correlate(): pl.pallas_call(functools.partial(correlate_kernel, windows, samples, lag_...  10.9 us

profile of v2, /device:TPU:1, one launch (start us, length us, event | category | flops | bytes accessed | tf_op | source)
XLA Modules:
  0.0 26.8 jit_solution(10248131821820979368)
XLA Ops:
  0.0 15.8 %prepare.1.ext_ref = bf16[416,256]{1,0:T(8,128)(2,1)} custom-call(bf16[1,64,1280]{2,1,0:T(8,128)(2,1)} %bitcast.3, bf16[1,64]{1,0:T(2,128)(2,1)} %bitcast.5, s32[1,160]{1,0:T(1,128)} %bitcast.4), custom_call_target="tpu_custom_call" | custom-call | tf_op jit(solution)/shard_map/prepare/pallas_call | solution.py:186
  15.8 10.9 %correlate.1 = bf16[160,128,256]{2,1,0:T(8,128)(2,1)} custom-call(bf16[416,256]{1,0:T(8,128)(2,1)} %prepare.1.ext_ref), custom_call_target="tpu_custom_call" | custom-call | tf_op jit(solution)/shard_map/correlate/pallas_call | solution.py:263

commit v3 on v2

--- a/solution.py
+++ b/solution.py
@@ -15,6 +15,7 @@
 HIST = 60
 LANES = 128
 SUB = 16
+VMEM_GRANT = 28 * 2**20
 MESH = pl.DeviceIdType.MESH
 
 
@@ -64,38 +65,57 @@
     outputs = tract_len // STRIDE
     reach = -(-OFF // channels)
 
+    def signal(chan, turn):
+        pl.semaphore_signal(
+            barrier,
+            inc=1,
+            device_id={"chan": chan, "tm": lax.rem(my_tm + turn, n_tm)},
+            device_id_type=MESH,
+        )
+
     barrier = pltpu.get_barrier_semaphore()
-    for step in range(n_chan):
-        for turn in range(n_tm):
-            if step or turn:
-                pl.semaphore_signal(
-                    barrier,
-                    inc=1,
-                    device_id={
-                        "chan": lax.rem(me + step, n_chan),
-                        "tm": lax.rem(my_tm + turn, n_tm),
-                    },
-                    device_id_type=MESH,
-                )
+    for step in range(1, n_chan):
+        signal(lax.rem(me + step, n_chan), 0)
+    for turn in range(1, n_tm):
+        signal(me, turn)
+        for k in range(1, reach + 1):
+
+            @pl.when(me >= k)
+            def _():
+                signal(me - k, turn)
+
+            @pl.when(me + k < n_chan)
+            def _():
+                signal(me + k, turn)
+
     turned = raw_ref[0].astype(jnp.float32).T.astype(jnp.bfloat16)
     for block in range(n_chan):
         first = block * channels
         pieces = [turned[first + m * part : first + (m + 1) * part] for m in range(members)]
         packed[block] = jnp.concatenate(pieces, axis=1)
-    pl.semaphore_wait(barrier, n_chan * n_tm - 1)
-
-    spread = []
-    for step in range(1, n_chan):
-        copy = pltpu.make_async_remote_copy(
-            src_ref=packed.at[lax.rem(me + step, n_chan)],
+    near_blocks = 1
+    for k in range(1, reach + 1):
+        near_blocks = near_blocks + (me + n_chan - k) // n_chan + 1 - (me + k) // n_chan
+    pl.semaphore_wait(barrier, n_chan - 1 + (n_tm - 1) * near_blocks)
+
+    def spread(target, slot):
+        return pltpu.make_async_remote_copy(
+            src_ref=packed.at[target],
             dst_ref=received.at[me],
-            send_sem=send_a.at[step],
-            recv_sem=recv_a.at[step],
-            device_id={"chan": lax.rem(me + step, n_chan)},
+            send_sem=send_a.at[slot],
+            recv_sem=recv_a.at[me],
+            device_id={"chan": target},
             device_id_type=MESH,
         )
-        copy.start()
-        spread.append(copy)
+
+    ways = [(distance, side) for distance in range(n_chan - 1, 0, -1) for side in range(2)]
+    for distance, side in ways:
+        target = me + distance if side else me - distance
+
+        @pl.when(target < n_chan if side else target >= 0)
+        def _():
+            spread(target, 2 * distance + side).start()
+
     received[me] = packed[me]
 
     fir[...] = jnp.zeros_like(fir)
@@ -125,8 +145,19 @@
                 (count, extended.shape[1]), extended.dtype
             )
 
-    for copy in spread:
-        copy.wait_recv()
+    for source in range(n_chan):
+
+        @pl.when(me != source)
+        def _():
+            pltpu.make_async_remote_copy(
+                src_ref=packed.at[source],
+                dst_ref=received.at[source],
+                send_sem=send_a.at[0],
+                recv_sem=recv_a.at[source],
+                device_id={"chan": source},
+                device_id_type=MESH,
+            ).wait_recv()
+
     tracts = jnp.concatenate([received[d] for d in range(n_chan)], axis=1)
     filtered = lax.dot_general(
         tracts, fir[...], (((1,), (1,)), ((), ())), preferred_element_type=jnp.float32
@@ -159,8 +190,13 @@
 
     own = pl.multiple_of(my_tm * samples, LANES)
     extended[0:channels, pl.ds(own, samples)] = white[...]
-    for copy in spread:
-        copy.wait_send()
+    for distance, side in ways:
+        target = me + distance if side else me - distance
+
+        @pl.when(target < n_chan if side else target >= 0)
+        def _():
+            spread(target, 2 * distance + side).wait_send()
+
     for k, turn in pairs:
 
         @pl.when(me + k < n_chan)
@@ -194,12 +230,14 @@
             pltpu.VMEM((members * samples, n_chan * width), jnp.bfloat16),
             pltpu.VMEM((channels, samples), jnp.bfloat16),
             pltpu.VMEM((channels + OFF, n_tm * samples), jnp.bfloat16),
-            pltpu.SemaphoreType.DMA((n_chan,)),
+            pltpu.SemaphoreType.DMA((2 * n_chan,)),
             pltpu.SemaphoreType.DMA((n_chan,)),
             pltpu.SemaphoreType.DMA((reach + 1, n_tm)),
             pltpu.SemaphoreType.DMA((reach + 1, n_tm)),
         ],
-        compiler_params=pltpu.CompilerParams(collective_id=0, has_side_effects=True),
+        compiler_params=pltpu.CompilerParams(
+            collective_id=0, has_side_effects=True, vmem_limit_bytes=VMEM_GRANT
+        ),
         name="prepare",
     )(raw_strain.transpose(0, 2, 1), fir_taps.reshape(1, TAPS), live_mask.reshape(1, channels))
 
@@ -267,6 +305,7 @@
         in_specs=[pl.BlockSpec(extended.shape, lambda g: (0, 0))],
         out_specs=pl.BlockSpec((SUB, lag_dev, OFF), lambda g: (g, 0, 0)),
         scratch_shapes=[pltpu.VMEM((channels - SUB + OFF + LANES, depth), jnp.bfloat16)],
+        compiler_params=pltpu.CompilerParams(vmem_limit_bytes=VMEM_GRANT),
         name="correlate",
     )(extended)
 

time: 26.9 us -> 26.7 us (level)
  Pallas kernels: 26.8 us -> 24.3 us
  local copies, waits for them, and re-layouts: 0 us -> 2.25 us
    unnamed x0 -> x6, local copies, waits for them, and re-layouts: none -> 2.25 us
    pallas_call x1, Pallas kernels: 15.8 us -> 14.3 us  [prepare(): pl.pallas_call(functools.partial(prepare_kernel, n_chan, n_tm, members),...]
    pallas_call x1, Pallas kernels: 10.9 us -> 10 us  [correlate(): pl.pallas_call(functools.partial(correlate_kernel, windows, samples, lag_...]
where the time goes in v3:
time: 26.7 us; the launch traced here: 26.6 us
  Pallas kernels  24.3 us (91%)
  local copies, waits for them, and re-layouts  2.25 us (8%)
    pallas_call x1, Pallas kernels, prepare(): pl.pallas_call(functools.partial(prepare_kernel, n_chan, n_tm, members),...  14.3 us
    pallas_call x1, Pallas kernels, correlate(): pl.pallas_call(functools.partial(correlate_kernel, windows, samples, lag_...  10 us
    unnamed x6, local copies, waits for them, and re-layouts  2.25 us

profile of v3, /device:TPU:1, one launch (start us, length us, event | category | flops | bytes accessed | tf_op | source)
XLA Modules:
  0.0 26.6 jit_solution(16652986412980407790)
XLA Ops:
  0.0 0.0 copy-start
  0.0 0.9 %copy-done = bf16[1,1280,64]{1,2,0:T(8,128)(2,1)S(1)} copy-done((bf16[1,1280,64]{1,2,0:T(8,128)(2,1)S(1)}, bf16[1,1280,64]{1,2,0:T(8,128)(2,1)}, u32[]{:S(2)}) %copy-start) | copy-done | bytes 163864
  0.9 0.0 copy-start.1
  0.9 0.7 %copy-done.1 = s32[160]{0:T(256)S(1)} copy-done((s32[160]{0:T(256)S(1)}, s32[160]{0:T(256)}, u32[]{:S(2)}) %copy-start.1) | copy-done | bytes 664
  1.6 0.0 copy-start.2
  1.6 0.7 %copy-done.2 = bf16[64]{0:T(256)(128)(2,1)S(1)} copy-done((bf16[64]{0:T(256)(128)(2,1)S(1)}, bf16[64]{0:T(256)(128)(2,1)}, u32[]{:S(2)}) %copy-start.2) | copy-done | bytes 152
  2.3 14.3 %prepare.1.ext_ref = bf16[416,256]{1,0:T(8,128)(2,1)S(1)} custom-call(bf16[1,64,1280]{2,1,0:T(8,128)(2,1)S(1)} %bitcast.3, bf16[1,64]{1,0:T(2,128)(2,1)S(1)} %bitcast.5, s32[1,160]{1,0:T(1,128)S(1)} %bitcast.4), custom_call_target="tpu_custom_call" | custom-call | tf_op jit(solution)/shard_map/prepare/pallas_call | solution.py:222
  16.6 10.0 %correlate.1 = bf16[160,128,256]{2,1,0:T(8,128)(2,1)} custom-call(bf16[416,256]{1,0:T(8,128)(2,1)S(1)} %prepare.1.ext_ref), custom_call_target="tpu_custom_call" | custom-call | tf_op jit(solution)/shard_map/correlate/pallas_call | solution.py:301
Async XLA Ops:
  0.0 0.9 %copy-start = (bf16[1,1280,64]{1,2,0:T(8,128)(2,1)S(1)}, bf16[1,1280,64]{1,2,0:T(8,128)(2,1)}, u32[]{:S(2)}) copy-start(bf16[1,1280,64]{1,2,0:T(8,128)(2,1)} %param.3) | copy-start | bytes 491524
  0.9 0.7 %copy-start.1 = (s32[160]{0:T(256)S(1)}, s32[160]{0:T(256)}, u32[]{:S(2)}) copy-start(s32[160]{0:T(256)} %param.5) | copy-start | bytes 1924
  1.6 0.7 %copy-start.2 = (bf16[64]{0:T(256)(128)(2,1)S(1)}, bf16[64]{0:T(256)(128)(2,1)}, u32[]{:S(2)}) copy-start(bf16[64]{0:T(256)(128)(2,1)} %param.4) | copy-start | bytes 388
